TPU v7x, 32 devices: a whole 2x2x4 slice. The times are simulated.
32 devices in a mesh: tile: 16 (over z, x, core), mem: 2 (over y).
Axes of the slice: x: 2, y: 2, z: 4, core: 2. Of those that a mesh axis runs over, the one named last changes fastest.
Arguments:
- ensemble: float32 [64, 7, 32768], P('mem', None, 'tile'), may hold values from -6 to 6
- obs_site: int32 [8, 32], replicated, may hold values from 0 to 14335
- obs_value: float32 [8, 32], replicated, may hold values from -8 to 8
- obs_var: float32 [8, 32], replicated, may hold values from 4 to 32
- owner_tile: int32 [8], replicated, may hold values from 0 to 15
- tile_mask: int32 [8, 16], replicated, may hold values 0 or 1
- batch_order: int32 [8], replicated, may hold values from 0 to 7, each once
Outputs:
- posterior: float32 [64, 7, 32768], P('mem', None, 'tile')
All inputs are finite; a program needn't handle non-finite values.
Results may differ from a plain program's by a relative error of at most 0.0001.
Values sent between devices are 32-bit elements; how exact they have to be, the bound alone decides.
No kernel may reach another device: no remote copies, remote signals or barrier semaphores. Data moves between devices by JAX's collectives and lax.ppermute only.
A program may use at most 64 MiB of HBM per device.

v0:
```python
import jax
import jax.numpy as jnp
from jax import lax
from jax.sharding import PartitionSpec as P

BATCHES = 8


def from_root(block, axis, holder):
    block = jnp.where(lax.axis_index(axis) == holder, block, jnp.zeros_like(block))
    return lax.psum(block, axis)


def batch_transform(priors, values, variances):
    count = priors.shape[1]
    highest = lax.Precision.HIGHEST

    def assimilate(transform, inputs):
        prior_row, value, variance = inputs
        y_row = jnp.dot(prior_row, transform, precision=highest)
        ens_mean = jnp.mean(y_row)
        spread = y_row - ens_mean
        sample_var = jnp.sum(spread * spread) / (count - 1)
        inv_total = 1.0 / (sample_var + variance)
        alpha = 1.0 / (1.0 + jnp.sqrt(variance * inv_total))
        weights = inv_total / (count - 1) * (value - ens_mean - alpha * spread)
        moved = jnp.dot(transform, spread, precision=highest)
        return (transform + moved[:, None] * weights[None, :], None)

    start_eye = jnp.eye(count, dtype=jnp.float32)
    result, _ = lax.scan(assimilate, start_eye, (priors, values, variances))
    return result


def body(ensemble, obs_site, obs_value, obs_var, owner_tile, tile_mask, batch_order):
    highest = lax.Precision.HIGHEST
    local_members = ensemble.shape[0]
    all_members = local_members * lax.axis_size("mem")
    tile_idx = lax.axis_index("tile")
    mem_idx = lax.axis_index("mem")
    flat_state = ensemble.reshape(local_members, -1)
    combined = jnp.eye(all_members, dtype=jnp.float32)
    for position in range(BATCHES):
        batch_id = batch_order[position]
        local_rows = jnp.take(flat_state, obs_site[batch_id], axis=1)
        obs_rows = lax.all_gather(local_rows, "mem", axis=0, tiled=True)
        own_priors = jnp.dot(obs_rows.T, combined, precision=highest)
        priors = from_root(own_priors, "tile", owner_tile[batch_id])
        transform = batch_transform(priors, obs_value[batch_id], obs_var[batch_id])
        updated = jnp.dot(combined, transform, precision=highest)
        combined = jnp.where(
            (tile_mask[batch_id, tile_idx] == 1) | (owner_tile[batch_id] == tile_idx),
            updated,
            combined,
        )
    my_columns = lax.dynamic_slice_in_dim(combined, mem_idx * local_members, local_members, 1)
    return jnp.einsum(
        "mn,mvc->nvc",
        my_columns,
        lax.all_gather(ensemble, "mem", axis=0, tiled=True),
        precision=highest,
    )


def solution(mesh):
    return jax.shard_map(
        body,
        mesh=mesh,
        in_specs=(P("mem", None, "tile"), P(), P(), P(), P(), P(), P()),
        out_specs=P("mem", None, "tile"),
        check_vma=False,
    )
```

profile of v0, /device:TPU:0, one launch (start us, length us, event | category | flops | bytes accessed | tf_op | source)
XLA Modules:
  0.0 2158.5 jit_solution(17621511112711468717)
XLA Ops:
  7.3 1.6 fusion.73
  18.7 6.0 copy.17
  39.2 3.7 gather_fusion
  43.0 5.8 all_gather.27
  49.0 61.2 %psum.56 = f32[32,64]{1,0:T(8,128)S(1)} all-reduce(f32[32,64]{1,0:T(8,128)S(1)} %convolution_select_fusion.14), channel_id=1, replica_groups=mesh['tile'=16,'mem'=2] {'tile'}, use_global_device_ids=true, to_apply=%region_0.0 | all-reduce | flops 2048 | bytes 16384 | tf_op jit(solution)/shard_map/psum | solution.py:11
  110.2 211.1 %while.80 = (s32[]{:T(128)}, f32[64,64]{1,0:T(8,128)S(1)}, f32[32,64]{1,0:T(8,128)S(1)}, f32[32]{0:T(128)S(1)}, f32[32]{0:T(128)S(1)}, /*index=5*/s32[]{:T(128)}, f32[]{:T(128)}, f32[]{:T(128)}, f32[]{:T(128)}) while((s32[]{:T(128)}, f32[64,64]{1,0:T(8,128)S(1)}, f32[32,64]{1,0:T(8,128)S(1)}, f32[32]{0:T(128)S(1)}, f32[32]{0:T(128)S(1)}, ...), condition=%wide.region_4.6_spmd, body=%wide.region_1.0_spmd.sunk | while | flops 107081 | bytes 84749 | solution.py:31
  321.3 3.7 gather_fusion.1
  325.2 4.4 all_gather.28
  331.3 57.6 %psum.57 = f32[32,64]{1,0:T(8,128)S(1)} all-reduce(f32[32,64]{1,0:T(8,128)S(1)} %convolution_select_fusion.13), channel_id=1, replica_groups=mesh['tile'=16,'mem'=2] {'tile'}, use_global_device_ids=true, to_apply=%region_5.7 | all-reduce | flops 2048 | bytes 16384 | tf_op jit(solution)/shard_map/psum | solution.py:11
  388.9 195.8 %while.81 = (s32[]{:T(128)}, f32[64,64]{1,0:T(8,128)S(1)}, f32[32,64]{1,0:T(8,128)S(1)}, f32[32]{0:T(128)S(1)}, f32[32]{0:T(128)S(1)}, /*index=5*/s32[]{:T(128)}, f32[]{:T(128)}, f32[]{:T(128)}, f32[]{:T(128)}) while((s32[]{:T(128)}, f32[64,64]{1,0:T(8,128)S(1)}, f32[32,64]{1,0:T(8,128)S(1)}, f32[32]{0:T(128)S(1)}, f32[32]{0:T(128)S(1)}, ...), condition=%wide.region_9.11_spmd, body=%wide.region_6.10_spmd.sunk | while | flops 107081 | bytes 84749 | solution.py:31
  585.4 3.7 gather_fusion.2
  589.2 4.4 all_gather.29
  594.1 57.6 %psum.58 = f32[32,64]{1,0:T(8,128)S(1)} all-reduce(f32[32,64]{1,0:T(8,128)S(1)} %convolution_select_fusion.12), channel_id=1, replica_groups=mesh['tile'=16,'mem'=2] {'tile'}, use_global_device_ids=true, to_apply=%region_10.12 | all-reduce | flops 2048 | bytes 16384 | tf_op jit(solution)/shard_map/psum | solution.py:11
  651.7 183.3 %while.82 = (s32[]{:T(128)}, f32[64,64]{1,0:T(8,128)S(1)}, f32[32,64]{1,0:T(8,128)S(1)}, f32[32]{0:T(128)S(1)}, f32[32]{0:T(128)S(1)}, /*index=5*/s32[]{:T(128)}, f32[]{:T(128)}, f32[]{:T(128)}, f32[]{:T(128)}) while((s32[]{:T(128)}, f32[64,64]{1,0:T(8,128)S(1)}, f32[32,64]{1,0:T(8,128)S(1)}, f32[32]{0:T(128)S(1)}, f32[32]{0:T(128)S(1)}, ...), condition=%wide.region_14.16_spmd, body=%wide.region_11.15_spmd.sunk | while | flops 107081 | bytes 84749 | solution.py:31
  835.7 3.7 gather_fusion.3
  839.5 4.4 all_gather.30
  844.4 57.6 %psum.59 = f32[32,64]{1,0:T(8,128)S(1)} all-reduce(f32[32,64]{1,0:T(8,128)S(1)} %convolution_select_fusion.11), channel_id=1, replica_groups=mesh['tile'=16,'mem'=2] {'tile'}, use_global_device_ids=true, to_apply=%region_15.17 | all-reduce | flops 2048 | bytes 16384 | tf_op jit(solution)/shard_map/psum | solution.py:11
  902.0 185.8 %while.83 = (s32[]{:T(128)}, f32[64,64]{1,0:T(8,128)S(1)}, f32[32,64]{1,0:T(8,128)S(1)}, f32[32]{0:T(128)S(1)}, f32[32]{0:T(128)S(1)}, /*index=5*/s32[]{:T(128)}, f32[]{:T(128)}, f32[]{:T(128)}, f32[]{:T(128)}) while((s32[]{:T(128)}, f32[64,64]{1,0:T(8,128)S(1)}, f32[32,64]{1,0:T(8,128)S(1)}, f32[32]{0:T(128)S(1)}, f32[32]{0:T(128)S(1)}, ...), condition=%wide.region_19.21_spmd, body=%wide.region_16.20_spmd.sunk | while | flops 107081 | bytes 84749 | solution.py:31
  1088.5 3.7 gather_fusion.4
  1092.3 4.4 all_gather.31
  1097.2 57.6 %psum.60 = f32[32,64]{1,0:T(8,128)S(1)} all-reduce(f32[32,64]{1,0:T(8,128)S(1)} %convolution_select_fusion.10), channel_id=1, replica_groups=mesh['tile'=16,'mem'=2] {'tile'}, use_global_device_ids=true, to_apply=%region_20.22 | all-reduce | flops 2048 | bytes 16384 | tf_op jit(solution)/shard_map/psum | solution.py:11
  1154.8 194.4 %while.84 = (s32[]{:T(128)}, f32[64,64]{1,0:T(8,128)S(1)}, f32[32,64]{1,0:T(8,128)S(1)}, f32[32]{0:T(128)S(1)}, f32[32]{0:T(128)S(1)}, /*index=5*/s32[]{:T(128)}, f32[]{:T(128)}, f32[]{:T(128)}, f32[]{:T(128)}) while((s32[]{:T(128)}, f32[64,64]{1,0:T(8,128)S(1)}, f32[32,64]{1,0:T(8,128)S(1)}, f32[32]{0:T(128)S(1)}, f32[32]{0:T(128)S(1)}, ...), condition=%wide.region_24.26_spmd, body=%wide.region_21.25_spmd.sunk | while | flops 107081 | bytes 84749 | solution.py:31
  1349.9 3.7 gather_fusion.5
  1353.7 4.4 all_gather.32
  1358.6 57.6 %psum.61 = f32[32,64]{1,0:T(8,128)S(1)} all-reduce(f32[32,64]{1,0:T(8,128)S(1)} %convolution_select_fusion.9), channel_id=1, replica_groups=mesh['tile'=16,'mem'=2] {'tile'}, use_global_device_ids=true, to_apply=%region_25.27 | all-reduce | flops 2048 | bytes 16384 | tf_op jit(solution)/shard_map/psum | solution.py:11
  1416.2 184.1 %while.85 = (s32[]{:T(128)}, f32[64,64]{1,0:T(8,128)S(1)}, f32[32,64]{1,0:T(8,128)S(1)}, f32[32]{0:T(128)S(1)}, f32[32]{0:T(128)S(1)}, /*index=5*/s32[]{:T(128)}, f32[]{:T(128)}, f32[]{:T(128)}, f32[]{:T(128)}) while((s32[]{:T(128)}, f32[64,64]{1,0:T(8,128)S(1)}, f32[32,64]{1,0:T(8,128)S(1)}, f32[32]{0:T(128)S(1)}, f32[32]{0:T(128)S(1)}, ...), condition=%wide.region_29.31_spmd, body=%wide.region_26.30_spmd.sunk | while | flops 107081 | bytes 84749 | solution.py:31
  1601.0 3.7 gather_fusion.6
  1604.8 4.4 all_gather.33
  1609.6 57.6 %psum.62 = f32[32,64]{1,0:T(8,128)S(1)} all-reduce(f32[32,64]{1,0:T(8,128)S(1)} %convolution_select_fusion.8), channel_id=1, replica_groups=mesh['tile'=16,'mem'=2] {'tile'}, use_global_device_ids=true, to_apply=%region_30.32 | all-reduce | flops 2048 | bytes 16384 | tf_op jit(solution)/shard_map/psum | solution.py:11
  1667.3 195.4 %while.86 = (s32[]{:T(128)}, f32[64,64]{1,0:T(8,128)S(1)}, f32[32,64]{1,0:T(8,128)S(1)}, f32[32]{0:T(128)S(1)}, f32[32]{0:T(128)S(1)}, /*index=5*/s32[]{:T(128)}, f32[]{:T(128)}, f32[]{:T(128)}, f32[]{:T(128)}) while((s32[]{:T(128)}, f32[64,64]{1,0:T(8,128)S(1)}, f32[32,64]{1,0:T(8,128)S(1)}, f32[32]{0:T(128)S(1)}, f32[32]{0:T(128)S(1)}, ...), condition=%wide.region_34.36_spmd, body=%wide.region_31.35_spmd.sunk | while | flops 107081 | bytes 84749 | solution.py:31
  1863.4 3.7 gather_fusion.7
  1867.3 4.4 all_gather.34
  1872.7 57.6 %psum.63 = f32[32,64]{1,0:T(8,128)S(1)} all-reduce(f32[32,64]{1,0:T(8,128)S(1)} %convolution_select_fusion.7), channel_id=1, replica_groups=mesh['tile'=16,'mem'=2] {'tile'}, use_global_device_ids=true, to_apply=%region_35.37 | all-reduce | flops 2048 | bytes 16384 | tf_op jit(solution)/shard_map/psum | solution.py:11
  1930.3 214.7 %while.87 = (s32[]{:T(128)}, f32[64,64]{1,0:T(8,128)S(1)}, f32[32,64]{1,0:T(8,128)S(1)}, f32[32]{0:T(128)S(1)}, f32[32]{0:T(128)S(1)}, /*index=5*/s32[]{:T(128)}, f32[]{:T(128)}, f32[]{:T(128)}, f32[]{:T(128)}) while((s32[]{:T(128)}, f32[64,64]{1,0:T(8,128)S(1)}, f32[32,64]{1,0:T(8,128)S(1)}, f32[32]{0:T(128)S(1)}, f32[32]{0:T(128)S(1)}, ...), condition=%wide.region_39.41_spmd, body=%wide.region_36.40_spmd.sunk | while | flops 107081 | bytes 84749 | solution.py:31
  1937.0 0.9 fusion.185
  1943.7 0.9 fusion.185
  1950.4 0.9 fusion.185
  1957.1 0.9 fusion.185
  1963.8 0.9 fusion.185
  1970.5 0.9 fusion.185
  1977.2 0.9 fusion.185
  1983.9 0.9 fusion.185
  1990.6 0.9 fusion.185
  1997.4 0.9 fusion.185
  2004.1 0.9 fusion.185
  2010.8 0.9 fusion.185
  2017.5 0.9 fusion.185
  2024.2 0.9 fusion.185
  2030.9 0.9 fusion.185
  2037.6 0.9 fusion.185
  2044.3 0.9 fusion.185
  2051.0 0.9 fusion.185
  2057.8 0.9 fusion.185
  2064.5 0.9 fusion.185
  2071.2 0.9 fusion.185
  2077.9 0.9 fusion.185
  2084.6 0.9 fusion.185
  2091.3 0.9 fusion.185
  2098.0 0.9 fusion.185
  2104.7 0.9 fusion.185
  2111.4 0.9 fusion.185
  2118.2 0.9 fusion.185
  2124.9 0.9 fusion.185
  2146.5 5.1 fusion.34
  (1829 shorter events, 724.3 us)
Async XLA Ops:
  6.5 23.1 %copy-start = (s32[8]{0:T(128)S(1)}, s32[8]{0:T(128)}, u32[]{:S(2)}) copy-start(s32[8]{0:T(128)} %param.29) | copy-start | bytes 100
  6.5 32.6 %copy-start.4 = (s32[8,32]{1,0:T(8,128)S(1)}, s32[8,32]{1,0:T(8,128)}, u32[]{:S(2)}) copy-start(s32[8,32]{1,0:T(8,128)} %param.26) | copy-start | bytes 3076
  6.5 103.7 %copy-start.2 = (f32[8,32]{1,0:T(8,128)S(1)}, f32[8,32]{1,0:T(8,128)}, u32[]{:S(2)}) copy-start(f32[8,32]{1,0:T(8,128)} %param.27) | copy-start | bytes 3076
  6.5 103.7 %copy-start.1 = (f32[8,32]{1,0:T(8,128)S(1)}, f32[8,32]{1,0:T(8,128)}, u32[]{:S(2)}) copy-start(f32[8,32]{1,0:T(8,128)} %param.28) | copy-start | bytes 3076
  6.5 323.0 %copy-start.3 = (s32[8,16]{1,0:T(8,128)S(1)}, s32[8,16]{1,0:T(8,128)}, u32[]{:S(2)}) copy-start(s32[8,16]{1,0:T(8,128)} %param.30) | copy-start | bytes 1540
  6.5 2140.0 %all-gather.2.cloned.1.call-start = ((), (), s32[]{:S(2)}) async-start(), calls=%async_computation | async-start | bytes 5505024 | tf_op jit(solution)/shard_map/all_gather | solution.py:60
Sparse Core Ops, SparseCore 0:
  8.9 53.8 all-gather.1
where the time goes:
time: 2170 us; the launch traced here: 2160 us
  loops' own time  822 us (38%)
  blocking collectives  501 us (23%)
  local copies, waits for them, and re-layouts  355 us (16%)
  matrix products  251 us (12%)
  other arithmetic  184 us (8%)
  between operations  43.6 us (2%)
    another operation x8, loops' own time, batch_transform(): result, _ = lax.scan(assimilate, start_eye, (priors, values, variances))  822 us
    psum x8, blocking collectives, from_root(): return lax.psum(block, axis)  465 us
    dynamic_slice x512, local copies, waits for them, and re-layouts, batch_transform(): result, _ = lax.scan(assimilate, start_eye, (priors, values, variances))  316 us
    dot_general x256, matrix products, assimilate(): y_row = jnp.dot(prior_row, transform, precision=highest)  207 us
    reduce_sum x256, other arithmetic, assimilate(): sample_var = jnp.sum(spread * spread) / (count - 1)  161 us
  transfers between devices with their start and end apart: 1, of which 0 were waited for; matrix products, arithmetic and copies ran while one was open for 36% of the time, Pallas kernels for 0%

commit v1 on v0

--- a/solution.py
+++ b/solution.py
@@ -8,7 +8,7 @@
 
 def from_root(block, axis, holder):
     block = jnp.where(lax.axis_index(axis) == holder, block, jnp.zeros_like(block))
-    return lax.psum(block, axis)
+    return jnp.sum(lax.all_gather(block, axis), axis=0)
 
 
 def batch_transform(priors, values, variances):

time: 2170 us -> 1860 us (0.86)
  blocking collectives: 501 us -> 191 us
    psum x8 -> x0, blocking collectives: 465 us -> none  [from_root(): return lax.psum(block, axis)]
    all_gather x0 -> x8, blocking collectives: none -> 154 us  [from_root(): return jnp.sum(lax.all_gather(block, axis), axis=0)]
  transfers between devices with their start and end apart: 1 -> 1, of which waited for: 0 -> 0; matrix products, arithmetic and copies ran while one was open for 36% -> 43% of each run, Pallas kernels for 0% -> 0%
where the time goes in v1:
time: 1860 us; the launch traced here: 1850 us
  loops' own time  822 us (44%)
  local copies, waits for them, and re-layouts  355 us (19%)
  matrix products  252 us (14%)
  blocking collectives  191 us (10%)
  other arithmetic  184 us (10%)
  between operations  43.6 us (2%)
    another operation x8, loops' own time, batch_transform(): result, _ = lax.scan(assimilate, start_eye, (priors, values, variances))  822 us
    dynamic_slice x512, local copies, waits for them, and re-layouts, batch_transform(): result, _ = lax.scan(assimilate, start_eye, (priors, values, variances))  316 us
    dot_general x256, matrix products, assimilate(): y_row = jnp.dot(prior_row, transform, precision=highest)  207 us
    reduce_sum x256, other arithmetic, assimilate(): sample_var = jnp.sum(spread * spread) / (count - 1)  161 us
    all_gather x8, blocking collectives, from_root(): return jnp.sum(lax.all_gather(block, axis), axis=0)  154 us
  transfers between devices with their start and end apart: 1, of which 0 were waited for; matrix products, arithmetic and copies ran while one was open for 43% of the time, Pallas kernels for 0%

profile of v1, /device:TPU:0, one launch (start us, length us, event | category | flops | bytes accessed | tf_op | source)
XLA Modules:
  0.0 1848.3 jit_solution(6882481702128962476)
XLA Ops:
  7.3 1.6 fusion.73
  18.7 6.0 copy.17
  39.2 3.7 gather_fusion
  43.0 5.8 all_gather.75
  49.0 22.9 %all-gather = f32[512,64]{1,0:T(8,128)S(1)} all-gather(f32[32,64]{1,0:T(8,128)S(1)} %convolution_select_fusion.14), channel_id=2, replica_groups=mesh['tile'=16,'mem'=2] {'tile'}, dimensions={0}, use_global_device_ids=true | all-gather | bytes 139264 | tf_op jit(solution)/shard_map/all_gather | solution.py:11
  71.9 211.1 %while.80 = (s32[]{:T(128)}, f32[64,64]{1,0:T(8,128)S(1)}, f32[32,64]{1,0:T(8,128)S(1)}, f32[32]{0:T(128)S(1)}, f32[32]{0:T(128)S(1)}, /*index=5*/s32[]{:T(128)}, f32[]{:T(128)}, f32[]{:T(128)}, f32[]{:T(128)}) while((s32[]{:T(128)}, f32[64,64]{1,0:T(8,128)S(1)}, f32[32,64]{1,0:T(8,128)S(1)}, f32[32]{0:T(128)S(1)}, f32[32]{0:T(128)S(1)}, ...), condition=%wide.region_4.6_spmd, body=%wide.region_1.0_spmd.sunk | while | flops 107081 | bytes 84749 | solution.py:31
  283.0 3.7 gather_fusion.1
  286.8 4.4 all_gather.78
  293.0 17.8 all-gather.1
  310.8 195.8 %while.81 = (s32[]{:T(128)}, f32[64,64]{1,0:T(8,128)S(1)}, f32[32,64]{1,0:T(8,128)S(1)}, f32[32]{0:T(128)S(1)}, f32[32]{0:T(128)S(1)}, /*index=5*/s32[]{:T(128)}, f32[]{:T(128)}, f32[]{:T(128)}, f32[]{:T(128)}) while((s32[]{:T(128)}, f32[64,64]{1,0:T(8,128)S(1)}, f32[32,64]{1,0:T(8,128)S(1)}, f32[32]{0:T(128)S(1)}, f32[32]{0:T(128)S(1)}, ...), condition=%wide.region_9.11_spmd, body=%wide.region_6.10_spmd.sunk | while | flops 107081 | bytes 84749 | solution.py:31
  507.4 3.7 gather_fusion.2
  511.2 4.4 all_gather.81
  516.0 19.9 %all-gather.2 = f32[512,64]{1,0:T(8,128)S(1)} all-gather(f32[32,64]{1,0:T(8,128)S(1)} %convolution_select_fusion.12), channel_id=4, replica_groups=mesh['tile'=16,'mem'=2] {'tile'}, dimensions={0}, use_global_device_ids=true | all-gather | bytes 139264 | tf_op jit(solution)/shard_map/all_gather | solution.py:11
  536.0 183.3 %while.82 = (s32[]{:T(128)}, f32[64,64]{1,0:T(8,128)S(1)}, f32[32,64]{1,0:T(8,128)S(1)}, f32[32]{0:T(128)S(1)}, f32[32]{0:T(128)S(1)}, /*index=5*/s32[]{:T(128)}, f32[]{:T(128)}, f32[]{:T(128)}, f32[]{:T(128)}) while((s32[]{:T(128)}, f32[64,64]{1,0:T(8,128)S(1)}, f32[32,64]{1,0:T(8,128)S(1)}, f32[32]{0:T(128)S(1)}, f32[32]{0:T(128)S(1)}, ...), condition=%wide.region_14.16_spmd, body=%wide.region_11.15_spmd.sunk | while | flops 107081 | bytes 84749 | solution.py:31
  720.0 3.7 gather_fusion.3
  723.8 4.4 all_gather.84
  728.7 17.8 all-gather.3
  746.6 185.8 %while.83 = (s32[]{:T(128)}, f32[64,64]{1,0:T(8,128)S(1)}, f32[32,64]{1,0:T(8,128)S(1)}, f32[32]{0:T(128)S(1)}, f32[32]{0:T(128)S(1)}, /*index=5*/s32[]{:T(128)}, f32[]{:T(128)}, f32[]{:T(128)}, f32[]{:T(128)}) while((s32[]{:T(128)}, f32[64,64]{1,0:T(8,128)S(1)}, f32[32,64]{1,0:T(8,128)S(1)}, f32[32]{0:T(128)S(1)}, f32[32]{0:T(128)S(1)}, ...), condition=%wide.region_19.21_spmd, body=%wide.region_16.20_spmd.sunk | while | flops 107081 | bytes 84749 | solution.py:31
  933.1 3.7 gather_fusion.4
  936.9 4.4 all_gather.87
  941.8 19.9 %all-gather.4 = f32[512,64]{1,0:T(8,128)S(1)} all-gather(f32[32,64]{1,0:T(8,128)S(1)} %convolution_select_fusion.10), channel_id=6, replica_groups=mesh['tile'=16,'mem'=2] {'tile'}, dimensions={0}, use_global_device_ids=true | all-gather | bytes 139264 | tf_op jit(solution)/shard_map/all_gather | solution.py:11
  961.7 194.4 %while.84 = (s32[]{:T(128)}, f32[64,64]{1,0:T(8,128)S(1)}, f32[32,64]{1,0:T(8,128)S(1)}, f32[32]{0:T(128)S(1)}, f32[32]{0:T(128)S(1)}, /*index=5*/s32[]{:T(128)}, f32[]{:T(128)}, f32[]{:T(128)}, f32[]{:T(128)}) while((s32[]{:T(128)}, f32[64,64]{1,0:T(8,128)S(1)}, f32[32,64]{1,0:T(8,128)S(1)}, f32[32]{0:T(128)S(1)}, f32[32]{0:T(128)S(1)}, ...), condition=%wide.region_24.26_spmd, body=%wide.region_21.25_spmd.sunk | while | flops 107081 | bytes 84749 | solution.py:31
  1156.8 3.7 gather_fusion.5
  1160.6 4.4 all_gather.90
  1165.5 17.8 all-gather.5
  1183.4 184.1 %while.85 = (s32[]{:T(128)}, f32[64,64]{1,0:T(8,128)S(1)}, f32[32,64]{1,0:T(8,128)S(1)}, f32[32]{0:T(128)S(1)}, f32[32]{0:T(128)S(1)}, /*index=5*/s32[]{:T(128)}, f32[]{:T(128)}, f32[]{:T(128)}, f32[]{:T(128)}) while((s32[]{:T(128)}, f32[64,64]{1,0:T(8,128)S(1)}, f32[32,64]{1,0:T(8,128)S(1)}, f32[32]{0:T(128)S(1)}, f32[32]{0:T(128)S(1)}, ...), condition=%wide.region_29.31_spmd, body=%wide.region_26.30_spmd.sunk | while | flops 107081 | bytes 84749 | solution.py:31
  1368.2 3.7 gather_fusion.6
  1372.0 4.4 all_gather.93
  1376.8 19.9 %all-gather.6 = f32[512,64]{1,0:T(8,128)S(1)} all-gather(f32[32,64]{1,0:T(8,128)S(1)} %convolution_select_fusion.8), channel_id=8, replica_groups=mesh['tile'=16,'mem'=2] {'tile'}, dimensions={0}, use_global_device_ids=true | all-gather | bytes 139264 | tf_op jit(solution)/shard_map/all_gather | solution.py:11
  1396.8 195.5 %while.86 = (s32[]{:T(128)}, f32[64,64]{1,0:T(8,128)S(1)}, f32[32,64]{1,0:T(8,128)S(1)}, f32[32]{0:T(128)S(1)}, f32[32]{0:T(128)S(1)}, /*index=5*/s32[]{:T(128)}, f32[]{:T(128)}, f32[]{:T(128)}, f32[]{:T(128)}) while((s32[]{:T(128)}, f32[64,64]{1,0:T(8,128)S(1)}, f32[32,64]{1,0:T(8,128)S(1)}, f32[32]{0:T(128)S(1)}, f32[32]{0:T(128)S(1)}, ...), condition=%wide.region_34.36_spmd, body=%wide.region_31.35_spmd.sunk | while | flops 107081 | bytes 84749 | solution.py:31
  1593.0 3.7 gather_fusion.7
  1596.8 4.4 all_gather.96
  1602.2 17.8 all-gather.7
  1620.1 214.7 %while.87 = (s32[]{:T(128)}, f32[64,64]{1,0:T(8,128)S(1)}, f32[32,64]{1,0:T(8,128)S(1)}, f32[32]{0:T(128)S(1)}, f32[32]{0:T(128)S(1)}, /*index=5*/s32[]{:T(128)}, f32[]{:T(128)}, f32[]{:T(128)}, f32[]{:T(128)}) while((s32[]{:T(128)}, f32[64,64]{1,0:T(8,128)S(1)}, f32[32,64]{1,0:T(8,128)S(1)}, f32[32]{0:T(128)S(1)}, f32[32]{0:T(128)S(1)}, ...), condition=%wide.region_39.41_spmd, body=%wide.region_36.40_spmd.sunk | while | flops 107081 | bytes 84749 | solution.py:31
  1626.8 0.9 fusion.185
  1633.5 0.9 fusion.185
  1640.2 0.9 fusion.185
  1646.9 0.9 fusion.185
  1653.6 0.9 fusion.185
  1660.3 0.9 fusion.185
  1667.0 0.9 fusion.185
  1673.8 0.9 fusion.185
  1680.5 0.9 fusion.185
  1687.2 0.9 fusion.185
  1693.9 0.9 fusion.185
  1700.6 0.9 fusion.185
  1707.3 0.9 fusion.185
  1714.0 0.9 fusion.185
  1720.7 0.9 fusion.185
  1727.4 0.9 fusion.185
  1734.2 0.9 fusion.185
  1740.9 0.9 fusion.185
  1747.6 0.9 fusion.185
  1754.3 0.9 fusion.185
  1761.0 0.9 fusion.185
  1767.7 0.9 fusion.185
  1774.4 0.9 fusion.185
  1781.1 0.9 fusion.185
  1787.8 0.9 fusion.185
  1794.6 0.9 fusion.185
  1801.3 0.9 fusion.185
  1808.0 0.9 fusion.185
  1821.4 0.9 fusion.185
  1836.3 5.1 fusion.34
  (1837 shorter events, 724.6 us)
Async XLA Ops:
  6.5 23.1 %copy-start = (s32[8]{0:T(128)S(1)}, s32[8]{0:T(128)}, u32[]{:S(2)}) copy-start(s32[8]{0:T(128)} %param.29) | copy-start | bytes 100
  6.5 32.6 %copy-start.4 = (s32[8,32]{1,0:T(8,128)S(1)}, s32[8,32]{1,0:T(8,128)}, u32[]{:S(2)}) copy-start(s32[8,32]{1,0:T(8,128)} %param.26) | copy-start | bytes 3076
  6.5 65.3 %copy-start.2 = (f32[8,32]{1,0:T(8,128)S(1)}, f32[8,32]{1,0:T(8,128)}, u32[]{:S(2)}) copy-start(f32[8,32]{1,0:T(8,128)} %param.27) | copy-start | bytes 3076
  6.5 65.4 %copy-start.1 = (f32[8,32]{1,0:T(8,128)S(1)}, f32[8,32]{1,0:T(8,128)}, u32[]{:S(2)}) copy-start(f32[8,32]{1,0:T(8,128)} %param.28) | copy-start | bytes 3076
  6.5 284.7 %copy-start.3 = (s32[8,16]{1,0:T(8,128)S(1)}, s32[8,16]{1,0:T(8,128)}, u32[]{:S(2)}) copy-start(s32[8,16]{1,0:T(8,128)} %param.30) | copy-start | bytes 1540
  6.5 1829.8 %all-gather.10.cloned.1.call-start = ((), (), s32[]{:S(2)}) async-start(), calls=%async_computation | async-start | bytes 5505024 | tf_op jit(solution)/shard_map/all_gather | solution.py:60
Sparse Core Ops, SparseCore 0:
  8.9 53.8 all-gather.9
